TPU v7x, 32 devices: a whole 2x2x4 slice. The times are simulated.
32 devices in a mesh: expert: 8 (over z, x), dp: 4 (over y, core).
Axes of the slice: x: 2, y: 2, z: 4, core: 2. Of those that a mesh axis runs over, the one named last changes fastest.
Arguments:
- enc_state: bfloat16 [4, 8, 256, 1024], P('dp', 'expert'), may hold values from -6 to 6
- baseline: bfloat16 [4, 8, 256, 1024], P('dp', 'expert'), may hold values from -6 to 6
- enc_keys: bfloat16 [4, 8, 256, 1024], P('dp', 'expert'), may hold values from -4 to 4
- dec_queries: bfloat16 [4, 8, 128, 1024], P('dp', 'expert'), may hold values from -200 to 200
- out_mult: bfloat16 [4, 8, 128, 1024], P('dp', 'expert'), may hold values from -6 to 6
- doc_lengths: int32 [4, 8], P('dp', 'expert'), may hold values from 128 to 256, as said below
- expert_ids: int32 [4, 8, 256], P('dp', 'expert'), may hold values from 0 to 15
- slot_ids: int32 [4, 8, 256], P('dp', 'expert'), may hold values from 0 to 31, as said below
- gate_prob: float32 [4, 8, 256], P('dp', 'expert'), may hold values from 0.2 to 1
- norm_gain: float32 [1024], replicated, may hold values from 0.5 to 2
- w_in: bfloat16 [16, 1024, 2816], P('expert', None, 'dp'), may hold values from -0.1875 to 0.1875
- w_out_t: bfloat16 [16, 1024, 2816], P('expert', None, 'dp'), may hold values from -0.109375 to 0.109375
- w_value: bfloat16 [1024, 1024], replicated, may hold values from -0.1875 to 0.1875
Outputs:
- enc_mult: bfloat16 [4, 8, 256, 1024], P('dp', 'expert')
Inputs may be any that keep to these rules, and one draw needn't show every extreme that they name: `slot_ids`: within one document no two tokens share an expert and a slot, and every token has a slot; one expert has all 32 slots used in every document. `doc_lengths`: some document has all 256 tokens.
All inputs are finite; a program needn't handle non-finite values.
Results may differ from a plain program's by a relative error of at most 0.0069.
Values may be sent and summed in bfloat16 or wider, within the bound.
A program may use at most 128 MiB of HBM per device.

v0:
```python
import math
import jax
import jax.numpy as jnp
from jax import lax
from jax.sharding import PartitionSpec as P

HEADS = 16
HEAD_DIM = 64


def rescale(pre_act, base_act):
    upper_part = jnp.maximum(jnp.maximum(pre_act, base_act), 0.0)
    lower_part = jnp.maximum(-jnp.minimum(pre_act, base_act), 0.0)
    return upper_part / (upper_part + lower_part + jnp.where(upper_part > 0.0, 0.0, 1.0))


def attend(query_rows, key_rows, mult_rows, length, w_value):
    enc_len = key_rows.shape[0]
    dec_len = query_rows.shape[0]
    queries = query_rows.reshape(dec_len, HEADS, HEAD_DIM)
    keys = key_rows.reshape(enc_len, HEADS, HEAD_DIM)
    mults = mult_rows.reshape(dec_len, HEADS, HEAD_DIM)
    scores = jnp.einsum("qhd,khd->hqk", queries, keys, preferred_element_type=jnp.float32) * (
        1.0 / math.sqrt(HEAD_DIM)
    )
    valid = jnp.arange(enc_len, dtype=jnp.int32) < length
    scores = jnp.where(valid[None, None, :], scores, -jnp.inf)
    top_score = jnp.max(scores, axis=-1, keepdims=True)
    expo = jnp.exp(scores - top_score)
    attn = (expo / jnp.sum(expo, axis=-1, keepdims=True)).astype(jnp.bfloat16)
    value_mult = jnp.einsum("hqk,qhd->khd", attn, mults, preferred_element_type=jnp.float32).astype(
        jnp.bfloat16
    )
    return lax.dot_general(
        value_mult.reshape(enc_len, HEADS * HEAD_DIM),
        w_value,
        (((1,), (1,)), ((), ())),
        preferred_element_type=jnp.float32,
    )


def expert_terms(rows_in, rows_base, rows_mult, part_in, part_out):
    pre_act = jnp.einsum("erd,edf->erf", rows_in, part_in, preferred_element_type=jnp.float32)
    base_act = jnp.einsum("erd,edf->erf", rows_base, part_in, preferred_element_type=jnp.float32)
    hidden_mult = jnp.einsum(
        "erd,edf->erf", rows_mult, part_out, preferred_element_type=jnp.float32
    )
    act_mult = (rescale(pre_act, base_act) * hidden_mult).astype(jnp.bfloat16)
    return jnp.einsum("erf,edf->erd", act_mult, part_in, preferred_element_type=jnp.float32)


def body(
    enc_state,
    baseline,
    enc_keys,
    dec_queries,
    out_mult,
    doc_lengths,
    expert_ids,
    slot_ids,
    gate_prob,
    norm_gain,
    w_in,
    w_out_t,
    w_value,
):
    enc_len = enc_state.shape[2]
    feature_width = enc_state.shape[3]
    local_experts = w_in.shape[0]
    n_experts = local_experts * lax.axis_size("expert")
    n_dp = lax.axis_size("dp")
    near = 2 if n_dp % 2 == 0 else 1
    capacity = max(2, 2 * enc_len // n_experts)
    shards = [(w_in, w_out_t)]
    if near == 2:
        swap = [(i, i ^ 1) for i in range(n_dp)]
        shards.append((lax.ppermute(w_in, "dp", swap), lax.ppermute(w_out_t, "dp", swap)))
    tokens = enc_state[0, 0].astype(jnp.float32)
    row_scale = norm_gain * lax.rsqrt(jnp.mean(tokens * tokens, axis=-1, keepdims=True) + 1e-06)
    inputs = (tokens * row_scale).astype(jnp.bfloat16)
    base_inputs = (baseline[0, 0].astype(jnp.float32) * row_scale).astype(jnp.bfloat16)
    flat_slot = expert_ids[0, 0] * capacity + slot_ids[0, 0]
    onehot = (
        flat_slot[None, :] == jnp.arange(n_experts * capacity, dtype=jnp.int32)[:, None]
    ).astype(jnp.bfloat16)

    def dispatch(values):
        placed = jnp.dot(onehot, values, preferred_element_type=jnp.float32).astype(jnp.bfloat16)
        placed = placed.reshape(n_experts, capacity, feature_width)
        return lax.all_to_all(placed, "expert", split_axis=0, concat_axis=1, tiled=True)

    sent_in = dispatch(inputs)
    sent_base = dispatch(base_inputs)
    layer_mult = attend(
        dec_queries[0, 0], enc_keys[0, 0], out_mult[0, 0], doc_lengths[0, 0], w_value
    )
    scaled_mult = (gate_prob[0, 0][:, None] * layer_mult).astype(jnp.bfloat16)
    sent_mult = dispatch(scaled_mult)
    own_rows = (sent_in, sent_base, sent_mult)

    def partial_sum(rows):
        total = expert_terms(*rows, *shards[0])
        for part in shards[1:]:
            total = total + expert_terms(*rows, *part)
        return total

    far = n_dp // near
    far_rows = []
    for hop in range(1, far):
        ahead = [(i, (i + hop * near) % n_dp) for i in range(n_dp)]
        far_rows.append(tuple((lax.ppermute(a, "dp", ahead) for a in own_rows)))
    slot_mult = partial_sum(own_rows)
    for hop in range(1, far):
        back = [((i + hop * near) % n_dp, i) for i in range(n_dp)]
        far_part = partial_sum(far_rows[hop - 1]).astype(jnp.bfloat16)
        slot_mult = slot_mult + lax.ppermute(far_part, "dp", back).astype(jnp.float32)
    returned = lax.all_to_all(
        slot_mult.astype(jnp.bfloat16), "expert", split_axis=1, concat_axis=0, tiled=True
    )
    per_token = lax.dot_general(
        onehot,
        returned.reshape(n_experts * capacity, feature_width),
        (((0,), (0,)), ((), ())),
        preferred_element_type=jnp.float32,
    )
    result = (layer_mult + row_scale * per_token).astype(jnp.bfloat16)
    return result[None, None]


def solution(mesh):
    in_specs = (
        P("dp", "expert", None, None),
        P("dp", "expert", None, None),
        P("dp", "expert", None, None),
        P("dp", "expert", None, None),
        P("dp", "expert", None, None),
        P("dp", "expert"),
        P("dp", "expert", None),
        P("dp", "expert", None),
        P("dp", "expert", None),
        P(),
        P("expert", None, "dp"),
        P("expert", None, "dp"),
        P(),
    )
    out_specs = P("dp", "expert", None, None)
    return jax.shard_map(body, mesh=mesh, in_specs=in_specs, out_specs=out_specs, check_vma=False)
```

profile of v0, /device:TPU:0, one launch (start us, length us, event | category | flops | bytes accessed | tf_op | source)
XLA Modules:
  0.0 234.2 jit_solution(12042869311677658196)
XLA Ops:
  0.0 0.0 copy-start
  0.0 1.4 copy.40
  1.4 1.1 copy.39
  3.2 1.1 copy.41
  4.3 2.0 fusion.48
  6.3 2.1 convolution_convert_fusion.3
  8.5 0.0 copy-start.5
  8.5 0.0 copy-start.6
  8.5 0.0 copy-start.4
  8.5 0.0 copy-done
  8.5 0.8 fusion.55
  9.3 0.0 copy-done.5
  9.3 0.0 copy-done.6
  9.4 0.0 copy-done.4
  9.4 0.0 copy-start.3
  9.4 1.5 convolution_convert_fusion
  10.9 7.3 %all-to-all-start.2 = ((bf16[16,32,1024]{2,1,0:T(8,128)(2,1)}), bf16[16,32,1024]{2,1,0:T(8,128)(2,1)}, u32[]{:S(2)}, u32[]{:S(2)}) async-start(bf16[16,32,1024]{2,1,0:T(8,128)(2,1)} %bitcast.78), calls=%async_computation.2 | async-start | bytes 2097152 | tf_op jit(solution)/shard_map/all_to_all | solution.py:90
  18.1 1.2 fusion.7
  19.4 0.0 copy-done.3
  19.4 2.6 %convolution_convert_fusion.2 = bf16[512,1024]{1,0:T(8,128)(2,1)} fusion(bf16[1,1,256,1024]{3,2,1,0:T(8,128)(2,1)} %param.13, f32[256]{0:T(256)S(1)} %add_rsqrt_fusion, f32[1024]{0:T(1024)S(1)} %copy-done.3, s32[256]{0:T(256)S(1)} %bitcast.88), kind=kOutput, calls=%fused_computation.12 | convolution fusion | flops 270139392 | bytes 1579008 | tf_op jit(solution)/shard_map/dot_general | solution.py:88
  22.0 22.0 %all-to-all-done.2 = bf16[16,32,1024]{2,1,0:T(8,128)(2,1)} async-done(((bf16[16,32,1024]{2,1,0:T(8,128)(2,1)}), bf16[16,32,1024]{2,1,0:T(8,128)(2,1)}, u32[]{:S(2)}, u32[]{:S(2)}) %all-to-all-start.2) | async-done | bytes 1048608 | tf_op jit(solution)/shard_map/all_to_all | solution.py:90
  44.0 4.2 %all-to-all-start = ((bf16[16,32,1024]{2,1,0:T(8,128)(2,1)}), bf16[16,32,1024]{2,1,0:T(8,128)(2,1)}, u32[]{:S(2)}, u32[]{:S(2)}) async-start(bf16[16,32,1024]{2,1,0:T(8,128)(2,1)} %bitcast.82), calls=%async_computation | async-start | bytes 2097152 | tf_op jit(solution)/shard_map/all_to_all | solution.py:90
  48.3 2.6 %convolution_convert_fusion.1 = bf16[512,1024]{1,0:T(8,128)(2,1)} fusion(bf16[1,1,256,1024]{3,2,1,0:T(8,128)(2,1)} %param.14, f32[256]{0:T(256)S(1)} %add_rsqrt_fusion, f32[1024]{0:T(1024)S(1)} %copy-done.3, s32[256]{0:T(256)S(1)} %bitcast.89), kind=kOutput, calls=%fused_computation.11 | convolution fusion | flops 270139392 | bytes 1579008 | tf_op jit(solution)/shard_map/dot_general | solution.py:88
  50.8 23.0 %all-to-all-done = bf16[16,32,1024]{2,1,0:T(8,128)(2,1)} async-done(((bf16[16,32,1024]{2,1,0:T(8,128)(2,1)}), bf16[16,32,1024]{2,1,0:T(8,128)(2,1)}, u32[]{:S(2)}, u32[]{:S(2)}) %all-to-all-start) | async-done | bytes 1048608 | tf_op jit(solution)/shard_map/all_to_all | solution.py:90
  73.8 4.4 %all-to-all-start.1 = ((bf16[16,32,1024]{2,1,0:T(8,128)(2,1)}), bf16[16,32,1024]{2,1,0:T(8,128)(2,1)}, u32[]{:S(2)}, u32[]{:S(2)}) async-start(bf16[16,32,1024]{2,1,0:T(8,128)(2,1)} %bitcast.81), calls=%async_computation.1 | async-start | bytes 2097152 | tf_op jit(solution)/shard_map/all_to_all | solution.py:90
  78.3 0.1 collective-permute-start
  78.4 0.5 collective-permute-start.1
  78.8 2.3 copy.44
  81.1 1.5 collective-permute-start.4
  82.7 2.3 copy.42
  85.0 0.5 collective-permute-start.2
  85.5 18.1 %all-to-all-done.1 = bf16[16,32,1024]{2,1,0:T(8,128)(2,1)} async-done(((bf16[16,32,1024]{2,1,0:T(8,128)(2,1)}), bf16[16,32,1024]{2,1,0:T(8,128)(2,1)}, u32[]{:S(2)}, u32[]{:S(2)}) %all-to-all-start.1) | async-done | bytes 1048608 | tf_op jit(solution)/shard_map/all_to_all | solution.py:90
  103.5 2.3 copy.43
  105.8 0.0 copy-start.1
  105.8 1.5 collective-permute-start.3
  107.3 4.3 %fusion.56 = f32[2,256,704]{1,2,0:T(8,128)} fusion(bf16[2,256,1024]{2,1,0:T(8,128)(2,1)} %bitcast.12, bf16[2,1024,704]{1,2,0:T(8,128)(2,1)} %param.23), kind=kOutput, calls=%fused_computation.72 | convolution fusion | flops 738197504 | bytes 5373952 | tf_op jit(solution)/shard_map/erd,edf->erf/dot_general | solution.py:43
  111.6 0.0 copy-done.1
  111.6 3.3 %fusion.57 = f32[2,256,704]{1,2,0:T(8,128)} fusion(bf16[2,256,1024]{2,1,0:T(8,128)(2,1)} %bitcast.17, bf16[2,1024,704]{1,2,0:T(8,128)(2,1)S(1)} %copy-done.1), kind=kOutput, calls=%fused_computation.73 | convolution fusion | flops 738197504 | bytes 5373952 | tf_op jit(solution)/shard_map/erd,edf->erf/dot_general | solution.py:44
  114.9 7.3 %fusion.6 = f32[2,256,1024]{2,1,0:T(8,128)} fusion(bf16[2,1024,704]{1,2,0:T(8,128)(2,1)} %param.23, bf16[2,256,1024]{2,1,0:T(8,128)(2,1)} %bitcast.22, bf16[2,1024,704]{1,2,0:T(8,128)(2,1)} %param.24, f32[2,256,704]{1,2,0:T(8,128)} %fusion.56, f32[2,256,704]{1,2,0:T(8,128)} %fusion.57), kind=kOutput, calls=%fused_computation.23 | convolution fusion | flops 1480720384 | bytes 11796480 | tf_op jit(solution)/shard_map/erf,edf->erd/dot_general | solution.py:49
  122.2 0.0 copy-start.2
  122.2 0.0 collective-permute-done
  122.2 4.3 %fusion.58 = f32[2,256,704]{1,2,0:T(8,128)} fusion(bf16[2,256,1024]{2,1,0:T(8,128)(2,1)} %bitcast.12, bf16[2,1024,704]{1,2,0:T(8,128)(2,1)} %collective-permute-done), kind=kOutput, calls=%fused_computation.74 | convolution fusion | flops 738197504 | bytes 5373952 | tf_op jit(solution)/shard_map/erd,edf->erf/dot_general | solution.py:43
  126.6 3.4 %collective-permute-done.2 = bf16[2,256,1024]{2,1,0:T(8,128)(2,1)} collective-permute-done((bf16[2,256,1024]{2,1,0:T(8,128)(2,1)}, bf16[2,256,1024]{2,1,0:T(8,128)(2,1)}, u32[]{:S(2)}, u32[]{:S(2)}) %collective-permute-start.2) | collective-permute-done | bytes 1048608 | tf_op jit(solution)/shard_map/ppermute | solution.py:111
  130.0 0.0 copy-done.2
  130.0 3.3 %fusion.60 = f32[2,256,704]{1,2,0:T(8,128)} fusion(bf16[2,256,1024]{2,1,0:T(8,128)(2,1)} %collective-permute-done.2, bf16[2,1024,704]{1,2,0:T(8,128)(2,1)S(1)} %copy-done.2), kind=kOutput, calls=%fused_computation.76 | convolution fusion | flops 738197504 | bytes 5373952 | tf_op jit(solution)/shard_map/erd,edf->erf/dot_general | solution.py:43
  133.2 4.2 %fusion.62 = f32[2,256,704]{1,2,0:T(8,128)} fusion(bf16[2,256,1024]{2,1,0:T(8,128)(2,1)} %collective-permute-done.2, bf16[2,1024,704]{1,2,0:T(8,128)(2,1)} %collective-permute-done), kind=kOutput, calls=%fused_computation.78 | convolution fusion | flops 738197504 | bytes 5373952 | tf_op jit(solution)/shard_map/erd,edf->erf/dot_general | solution.py:43
  137.5 14.1 %collective-permute-done.3 = bf16[2,256,1024]{2,1,0:T(8,128)(2,1)} collective-permute-done((bf16[2,256,1024]{2,1,0:T(8,128)(2,1)}, bf16[2,256,1024]{2,1,0:T(8,128)(2,1)}, u32[]{:S(2)}, u32[]{:S(2)}) %collective-permute-start.3) | collective-permute-done | bytes 1048608 | tf_op jit(solution)/shard_map/ppermute | solution.py:111
  151.5 3.3 %fusion.61 = f32[2,256,704]{1,2,0:T(8,128)} fusion(bf16[2,256,1024]{2,1,0:T(8,128)(2,1)} %collective-permute-done.3, bf16[2,1024,704]{1,2,0:T(8,128)(2,1)S(1)} %copy-done.2), kind=kOutput, calls=%fused_computation.77 | convolution fusion | flops 738197504 | bytes 5373952 | tf_op jit(solution)/shard_map/erd,edf->erf/dot_general | solution.py:44
  154.8 4.2 %fusion.63 = f32[2,256,704]{1,2,0:T(8,128)} fusion(bf16[2,256,1024]{2,1,0:T(8,128)(2,1)} %collective-permute-done.3, bf16[2,1024,704]{1,2,0:T(8,128)(2,1)} %collective-permute-done), kind=kOutput, calls=%fused_computation.79 | convolution fusion | flops 738197504 | bytes 5373952 | tf_op jit(solution)/shard_map/erd,edf->erf/dot_general | solution.py:44
  159.0 0.0 collective-permute-done.4
  159.0 7.4 %fusion.14 = f32[2,256,1024]{2,1,0:T(8,128)} fusion(bf16[2,1024,704]{1,2,0:T(8,128)(2,1)} %param.23, f32[2,256,704]{1,2,0:T(8,128)} %fusion.60, f32[2,256,704]{1,2,0:T(8,128)} %fusion.61, bf16[2,256,1024]{2,1,0:T(8,128)(2,1)} %collective-permute-done.4, bf16[2,1024,704]{1,2,0:T(8,128)(2,1)} %param.24), kind=kOutput, calls=%fused_computation.32 | convolution fusion | flops 1480720384 | bytes 11796480 | tf_op jit(solution)/shard_map/erf,edf->erd/dot_general | solution.py:49
  166.4 0.0 collective-permute-done.1
  166.4 7.8 %add_convert_fusion.1 = bf16[2,256,1024]{2,1,0:T(8,128)(2,1)} fusion(f32[2,256,1024]{2,1,0:T(8,128)} %fusion.14, bf16[2,1024,704]{1,2,0:T(8,128)(2,1)} %collective-permute-done, f32[2,256,704]{1,2,0:T(8,128)} %fusion.62, f32[2,256,704]{1,2,0:T(8,128)} %fusion.63, bf16[2,256,1024]{2,1,0:T(8,128)(2,1)} %collective-permute-done.4, ...), kind=kOutput, calls=%fused_computation.2 | convolution fusion | flops 1481768960 | bytes 12845056 | tf_op jit(solution)/shard_map/erf,edf->erd/dot_general | solution.py:49
  174.2 1.5 collective-permute-start.5
  175.7 4.2 %fusion.59 = f32[2,256,704]{1,2,0:T(8,128)} fusion(bf16[2,256,1024]{2,1,0:T(8,128)(2,1)} %bitcast.17, bf16[2,1024,704]{1,2,0:T(8,128)(2,1)} %collective-permute-done), kind=kOutput, calls=%fused_computation.75 | convolution fusion | flops 738197504 | bytes 5373952 | tf_op jit(solution)/shard_map/erd,edf->erf/dot_general | solution.py:44
  179.9 7.4 %fusion.13 = f32[2,256,1024]{2,1,0:T(8,128)} fusion(bf16[2,1024,704]{1,2,0:T(8,128)(2,1)} %collective-permute-done, f32[2,256,704]{1,2,0:T(8,128)} %fusion.58, f32[2,256,704]{1,2,0:T(8,128)} %fusion.59, bf16[2,256,1024]{2,1,0:T(8,128)(2,1)} %bitcast.22, bf16[2,1024,704]{1,2,0:T(8,128)(2,1)} %collective-permute-done.1), kind=kOutput, calls=%fused_computation.31 | convolution fusion | flops 1480720384 | bytes 11796480 | tf_op jit(solution)/shard_map/erf,edf->erd/dot_general | solution.py:49
  187.3 11.5 %collective-permute-done.5 = bf16[2,256,1024]{2,1,0:T(8,128)(2,1)} collective-permute-done((bf16[2,256,1024]{2,1,0:T(8,128)(2,1)}, bf16[2,256,1024]{2,1,0:T(8,128)(2,1)}, u32[]{:S(2)}, u32[]{:S(2)}) %collective-permute-start.5) | collective-permute-done | bytes 1048608 | tf_op jit(solution)/shard_map/ppermute | solution.py:116
  198.8 3.1 %add_convert_fusion = bf16[2,256,1024]{2,1,0:T(8,128)(2,1)S(1)} fusion(bf16[2,256,1024]{2,1,0:T(8,128)(2,1)} %collective-permute-done.5, f32[2,256,1024]{2,1,0:T(8,128)} %fusion.6, f32[2,256,1024]{2,1,0:T(8,128)} %fusion.13), kind=kLoop, calls=%fused_computation.1 | loop fusion | flops 2097152 | bytes 6291456 | tf_op jit(solution)/shard_map/convert_element_type | solution.py:118
  202.0 1.1 copy.45
  203.0 29.5 %all_to_all.69 = bf16[2,256,1024]{2,0,1:T(2,128)(2,1)S(1)} all-to-all(bf16[2,256,1024]{2,0,1:T(2,128)(2,1)S(1)} %copy.45), channel_id=1, replica_groups=mesh['expert'=8,'dp'=4] {'expert'}, dimensions={1} | all-to-all | bytes 2097152 | tf_op jit(solution)/shard_map/all_to_all | solution.py:117
  232.5 0.3 copy.46
  232.8 0.1 copy.47
  232.9 1.3 fusion.5
  (3 shorter events, 0.0 us)
Async XLA Ops:
  0.0 8.5 %copy-start = (bf16[1024,1024]{1,0:T(8,128)(2,1)S(1)}, bf16[1024,1024]{1,0:T(8,128)(2,1)}, u32[]{:S(2)}) copy-start(bf16[1024,1024]{1,0:T(8,128)(2,1)} %param.25) | copy-start | bytes 6291460
  8.5 0.8 copy-start.5
  8.5 0.8 copy-start.6
  8.5 0.8 copy-start.4
  9.4 10.0 %copy-start.3 = (f32[1024]{0:T(1024)S(1)}, f32[1024]{0:T(1024)}, u32[]{:S(2)}) copy-start(f32[1024]{0:T(1024)} %param.22) | copy-start | bytes 12292
  10.9 33.2 %all-to-all-start.2 = ((bf16[16,32,1024]{2,1,0:T(8,128)(2,1)}), bf16[16,32,1024]{2,1,0:T(8,128)(2,1)}, u32[]{:S(2)}, u32[]{:S(2)}) async-start(bf16[16,32,1024]{2,1,0:T(8,128)(2,1)} %bitcast.78), calls=%async_computation.2 | async-start | bytes 2097152 | tf_op jit(solution)/shard_map/all_to_all | solution.py:90
  44.0 29.8 %all-to-all-start = ((bf16[16,32,1024]{2,1,0:T(8,128)(2,1)}), bf16[16,32,1024]{2,1,0:T(8,128)(2,1)}, u32[]{:S(2)}, u32[]{:S(2)}) async-start(bf16[16,32,1024]{2,1,0:T(8,128)(2,1)} %bitcast.82), calls=%async_computation | async-start | bytes 2097152 | tf_op jit(solution)/shard_map/all_to_all | solution.py:90
  73.8 29.7 %all-to-all-start.1 = ((bf16[16,32,1024]{2,1,0:T(8,128)(2,1)}), bf16[16,32,1024]{2,1,0:T(8,128)(2,1)}, u32[]{:S(2)}, u32[]{:S(2)}) async-start(bf16[16,32,1024]{2,1,0:T(8,128)(2,1)} %bitcast.81), calls=%async_computation.1 | async-start | bytes 2097152 | tf_op jit(solution)/shard_map/all_to_all | solution.py:90
  78.3 44.0 %collective-permute-start = (bf16[2,1024,704]{1,2,0:T(8,128)(2,1)}, bf16[2,1024,704]{1,2,0:T(8,128)(2,1)}, u32[]{:S(2)}, u32[]{:S(2)}) collective-permute-start(bf16[2,1024,704]{1,2,0:T(8,128)(2,1)} %param.23), channel_id=1, source_target_pairs={{0,1},{1,0},{2,3},{3,2},{4,5},{5,4},{6,7},{7,6},{8,9},{9,8},{10,11... | collective-permute-start | bytes 8650760 | tf_op jit(solution)/shard_map/ppermute | solution.py:77
  78.4 88.1 %collective-permute-start.1 = (bf16[2,1024,704]{1,2,0:T(8,128)(2,1)}, bf16[2,1024,704]{1,2,0:T(8,128)(2,1)}, u32[]{:S(2)}, u32[]{:S(2)}) collective-permute-start(bf16[2,1024,704]{1,2,0:T(8,128)(2,1)} %param.24), channel_id=1, source_target_pairs={{0,1},{1,0},{2,3},{3,2},{4,5},{5,4},{6,7},{7,6},{8,9},{9,8},{10,11... | collective-permute-start | bytes 8650760 | tf_op jit(solution)/shard_map/ppermute | solution.py:77
  81.1 77.9 %collective-permute-start.4 = (bf16[2,256,1024]{2,1,0:T(8,128)(2,1)}, bf16[2,256,1024]{2,1,0:T(8,128)(2,1)}, u32[]{:S(2)}, u32[]{:S(2)}) collective-permute-start(bf16[2,256,1024]{2,1,0:T(8,128)(2,1)} %bitcast.22), channel_id=1, source_target_pairs={{0,2},{1,3},{2,0},{3,1},{4,6},{5,7},{6,4},{7,5},{8,10},{9,11},{10,... | collective-permute-start | bytes 3145736 | tf_op jit(solution)/shard_map/ppermute | solution.py:111
  85.0 45.0 %collective-permute-start.2 = (bf16[2,256,1024]{2,1,0:T(8,128)(2,1)}, bf16[2,256,1024]{2,1,0:T(8,128)(2,1)}, u32[]{:S(2)}, u32[]{:S(2)}) collective-permute-start(bf16[2,256,1024]{2,1,0:T(8,128)(2,1)} %bitcast.12), channel_id=1, source_target_pairs={{0,2},{1,3},{2,0},{3,1},{4,6},{5,7},{6,4},{7,5},{8,10},{9,11},{10,... | collective-permute-start | bytes 3145736 | tf_op jit(solution)/shard_map/ppermute | solution.py:111
  105.8 5.8 %copy-start.1 = (bf16[2,1024,704]{1,2,0:T(8,128)(2,1)S(1)}, bf16[2,1024,704]{1,2,0:T(8,128)(2,1)}, u32[]{:S(2)}) copy-start(bf16[2,1024,704]{1,2,0:T(8,128)(2,1)} %param.23) | copy-start | bytes 8650756
  105.8 45.7 %collective-permute-start.3 = (bf16[2,256,1024]{2,1,0:T(8,128)(2,1)}, bf16[2,256,1024]{2,1,0:T(8,128)(2,1)}, u32[]{:S(2)}, u32[]{:S(2)}) collective-permute-start(bf16[2,256,1024]{2,1,0:T(8,128)(2,1)} %bitcast.17), channel_id=1, source_target_pairs={{0,2},{1,3},{2,0},{3,1},{4,6},{5,7},{6,4},{7,5},{8,10},{9,11},{10,... | collective-permute-start | bytes 3145736 | tf_op jit(solution)/shard_map/ppermute | solution.py:111
  122.2 7.7 %copy-start.2 = (bf16[2,1024,704]{1,2,0:T(8,128)(2,1)S(1)}, bf16[2,1024,704]{1,2,0:T(8,128)(2,1)}, u32[]{:S(2)}) copy-start(bf16[2,1024,704]{1,2,0:T(8,128)(2,1)} %param.23) | copy-start | bytes 8650756
  174.2 24.6 %collective-permute-start.5 = (bf16[2,256,1024]{2,1,0:T(8,128)(2,1)}, bf16[2,256,1024]{2,1,0:T(8,128)(2,1)}, u32[]{:S(2)}, u32[]{:S(2)}) collective-permute-start(bf16[2,256,1024]{2,1,0:T(8,128)(2,1)} %add_convert_fusion.1), channel_id=1, source_target_pairs={{2,0},{3,1},{0,2},{1,3},{6,4},{7,5},{4,6},{5,7},{10,8},{11,9},{8,1... | collective-permute-start | bytes 3145736 | tf_op jit(solution)/shard_map/ppermute | solution.py:116
where the time goes:
time: 235 us; the launch traced here: 234 us
  waiting for transfers between devices  92.1 us (39%)
  matrix products  73.8 us (31%)
  blocking collectives  29.5 us (13%)
  starting transfers between devices  21.6 us (9%)
  local copies, waits for them, and re-layouts  12 us (5%)
  other arithmetic  4.38 us (2%)
    all_to_all x3, waiting for transfers between devices, dispatch(): lax.all_to_all(placed, 'expert', split_axis=0, concat_axis=1, tiled=True)  63.1 us
    dot_general x4, matrix products, expert_terms(): jnp.einsum('erf,edf->erd', act_mult, part_in, preferred_element_type=jnp....  29.8 us
    all_to_all x1, blocking collectives, body(): lax.all_to_all(slot_mult.astype(jnp.bfloat16), 'expert', split_axis=1, co...  29.5 us
    ppermute x3, waiting for transfers between devices, body(): far_rows.append(tuple((lax.ppermute(a, 'dp', ahead) for a in own_rows)))  17.5 us
    dot_general x4, matrix products, expert_terms(): jnp.einsum('erd,edf->erf', rows_in, part_in, preferred_element_type=jnp.f...  16.1 us
    all_to_all x3, starting transfers between devices, dispatch(): lax.all_to_all(placed, 'expert', split_axis=0, concat_axis=1, tiled=True)  15.9 us
    dot_general x4, matrix products, expert_terms(): jnp.einsum('erd,edf->erf', rows_base, part_in, preferred_element_type=jnp...  15 us
    ppermute x1, waiting for transfers between devices, body(): lax.ppermute(far_part, 'dp', back).astype(jnp.float32)  11.5 us
  transfers between devices with their start and end apart: 9, of which 6 were waited for; matrix products, arithmetic and copies ran while one was open for 28% of the time, Pallas kernels for 0%

commit v1 on v0

--- a/solution.py
+++ b/solution.py
@@ -6,6 +6,12 @@
 
 HEADS = 16
 HEAD_DIM = 64
+
+
+def exchange_blocks(array, name, split, join):
+    pieces = jnp.split(array, lax.axis_size(name), axis=split)
+    received = lax.all_to_all(jnp.stack(pieces), name, 0, 0)
+    return jnp.concatenate(received, axis=join)
 
 
 def rescale(pre_act, base_act):
@@ -87,7 +93,7 @@
     def dispatch(values):
         placed = jnp.dot(onehot, values, preferred_element_type=jnp.float32).astype(jnp.bfloat16)
         placed = placed.reshape(n_experts, capacity, feature_width)
-        return lax.all_to_all(placed, "expert", split_axis=0, concat_axis=1, tiled=True)
+        return exchange_blocks(placed, "expert", 0, 1)
 
     sent_in = dispatch(inputs)
     sent_base = dispatch(base_inputs)

time: 235 us -> 226 us (0.962)
  waiting for transfers between devices: 92.1 us -> 66.5 us
  local copies, waits for them, and re-layouts: 12 us -> 29.1 us
    all_to_all x3, waiting for transfers between devices: 63.1 us -> 45 us  [exchange_blocks(): received = lax.all_to_all(jnp.stack(pieces), name, 0, 0)]
    unnamed x17 -> x40, local copies, waits for them, and re-layouts: 3.67 us -> 18.5 us
    ppermute x3, waiting for transfers between devices: 17.5 us -> 9.98 us  [body(): far_rows.append(tuple((lax.ppermute(a, 'dp', ahead) for a in own_rows)))]
    reshape x0 -> x2, local copies, waits for them, and re-layouts: none -> 4.61 us  [exchange_blocks(): return jnp.concatenate(received, axis=join)]
    all_to_all x3 -> x1, local copies, waits for them, and re-layouts: 6.87 us -> 2.29 us  [exchange_blocks(): received = lax.all_to_all(jnp.stack(pieces), name, 0, 0)]
    dot_general x3, matrix products: 6.64 us -> 3.72 us  [dispatch(): jnp.dot(onehot, values, preferred_element_type=jnp.float32)]
  transfers between devices with their start and end apart: 9 -> 9, of which waited for: 6 -> 5; matrix products, arithmetic and copies ran while one was open for 28% -> 37% of each run, Pallas kernels for 0% -> 0%
where the time goes in v1:
time: 226 us; the launch traced here: 225 us
  matrix products  72.1 us (32%)
  waiting for transfers between devices  66.5 us (29%)
  blocking collectives  29.5 us (13%)
  local copies, waits for them, and re-layouts  29.1 us (13%)
  starting transfers between devices  21.7 us (10%)
  other arithmetic  5.23 us (2%)
    all_to_all x3, waiting for transfers between devices, exchange_blocks(): received = lax.all_to_all(jnp.stack(pieces), name, 0, 0)  45 us
    dot_general x4, matrix products, expert_terms(): jnp.einsum('erf,edf->erd', act_mult, part_in, preferred_element_type=jnp....  29.8 us
    all_to_all x1, blocking collectives, body(): lax.all_to_all(slot_mult.astype(jnp.bfloat16), 'expert', split_axis=1, co...  29.5 us
    unnamed x40, local copies, waits for them, and re-layouts  18.5 us
    dot_general x4, matrix products, expert_terms(): jnp.einsum('erd,edf->erf', rows_in, part_in, preferred_element_type=jnp.f...  16.1 us
    all_to_all x3, starting transfers between devices, exchange_blocks(): received = lax.all_to_all(jnp.stack(pieces), name, 0, 0)  16.1 us
    dot_general x4, matrix products, expert_terms(): jnp.einsum('erd,edf->erf', rows_base, part_in, preferred_element_type=jnp...  15 us
    ppermute x1, waiting for transfers between devices, body(): lax.ppermute(far_part, 'dp', back).astype(jnp.float32)  11.5 us
  transfers between devices with their start and end apart: 9, of which 5 were waited for; matrix products, arithmetic and copies ran while one was open for 37% of the time, Pallas kernels for 0%

profile of v1, /device:TPU:0, one launch (start us, length us, event | category | flops | bytes accessed | tf_op | source)
XLA Modules:
  0.0 225.0 jit_solution(15283952869562136812)
XLA Ops:
  0.0 1.4 fusion.7
  1.4 0.7 multiply_add_fusion
  2.1 1.6 convolution_convert_fusion.2
  3.8 0.7 constant_dynamic-update-slice_fusion.7
  4.5 0.7 constant_dynamic-update-slice_fusion.6
  5.1 0.6 constant_dynamic-update-slice_fusion.5
  5.8 0.7 constant_dynamic-update-slice_fusion.4
  6.4 0.7 constant_dynamic-update-slice_fusion.3
  7.1 0.7 constant_dynamic-update-slice_fusion.2
  7.8 0.7 constant_dynamic-update-slice_fusion.1
  8.4 0.7 constant_dynamic-update-slice_fusion
  9.1 7.4 %all-to-all-start = ((bf16[8,2,32,1024]{3,2,1,0:T(8,128)(2,1)}), bf16[8,2,32,1024]{3,2,1,0:T(8,128)(2,1)S(1)}, u32[]{:S(2)}, u32[]{:S(2)}) async-start(bf16[8,2,32,1024]{3,2,1,0:T(8,128)(2,1)} %constant_dynamic-update-slice_fusion), calls=%async_computation | async-start | bytes 2097152 | tf_op jit(solution)/shard_map/all_to_all | solution.py:13
  16.5 0.8 copy.42
  18.0 1.8 copy.40
  19.8 2.0 copy.41
  21.8 1.6 convolution_convert_fusion.1
  23.6 0.7 constant_dynamic-update-slice_fusion.15
  24.2 0.7 constant_dynamic-update-slice_fusion.14
  24.9 0.6 constant_dynamic-update-slice_fusion.13
  25.5 0.7 constant_dynamic-update-slice_fusion.12
  26.2 0.6 constant_dynamic-update-slice_fusion.11
  26.8 0.7 constant_dynamic-update-slice_fusion.10
  27.5 0.7 constant_dynamic-update-slice_fusion.9
  28.1 0.6 constant_dynamic-update-slice_fusion.8
  28.8 3.2 %fusion.51 = (f32[16,128]{1,0:T(8,128)S(1)}, f32[16,128,256]{2,1,0:T(8,128)}) fusion(pred[256]{0:T(512)(128)(4,1)S(1)} %iota_compare_fusion.5, bf16[128,16,64]{0,2,1:T(8,128)(2,1)} %bitcast.124, bf16[256,16,64]{0,2,1:T(8,128)(2,1)} %bitcast.122), kind=kOutput, calls=%fused_computation.94 | convolution fusion | flops 69206272 | bytes 2892032 | tf_op jit(solution)/shard_map/sub | solution.py:35
  32.0 10.3 %all-to-all-done = bf16[8,2,32,1024]{3,2,1,0:T(8,128)(2,1)S(1)} async-done(((bf16[8,2,32,1024]{3,2,1,0:T(8,128)(2,1)}), bf16[8,2,32,1024]{3,2,1,0:T(8,128)(2,1)S(1)}, u32[]{:S(2)}, u32[]{:S(2)}) %all-to-all-start) | async-done | bytes 1048608 | tf_op jit(solution)/shard_map/all_to_all | solution.py:13
  42.3 4.2 %all-to-all-start.1 = ((bf16[8,2,32,1024]{3,2,1,0:T(8,128)(2,1)}), bf16[8,2,32,1024]{3,2,1,0:T(8,128)(2,1)}, u32[]{:S(2)}, u32[]{:S(2)}) async-start(bf16[8,2,32,1024]{3,2,1,0:T(8,128)(2,1)} %constant_dynamic-update-slice_fusion.8), calls=%async_computation.1 | async-start | bytes 2097152 | tf_op jit(solution)/shard_map/all_to_all | solution.py:13
  46.5 2.1 convolution_convert_fusion.3
  48.7 0.8 fusion.58
  50.1 0.7 constant_dynamic-update-slice_fusion.23
  50.8 0.7 constant_dynamic-update-slice_fusion.22
  51.4 0.7 constant_dynamic-update-slice_fusion.21
  52.1 0.7 constant_dynamic-update-slice_fusion.20
  52.8 0.7 constant_dynamic-update-slice_fusion.19
  53.4 0.7 constant_dynamic-update-slice_fusion.18
  54.1 0.7 constant_dynamic-update-slice_fusion.17
  54.7 0.6 constant_dynamic-update-slice_fusion.16
  55.4 16.7 %all-to-all-done.1 = bf16[8,2,32,1024]{3,2,1,0:T(8,128)(2,1)} async-done(((bf16[8,2,32,1024]{3,2,1,0:T(8,128)(2,1)}), bf16[8,2,32,1024]{3,2,1,0:T(8,128)(2,1)}, u32[]{:S(2)}, u32[]{:S(2)}) %all-to-all-start.1) | async-done | bytes 1048608 | tf_op jit(solution)/shard_map/all_to_all | solution.py:13
  72.1 4.4 %all-to-all-start.2 = ((bf16[8,2,32,1024]{3,2,1,0:T(8,128)(2,1)}), bf16[8,2,32,1024]{3,2,1,0:T(8,128)(2,1)}, u32[]{:S(2)}, u32[]{:S(2)}) async-start(bf16[8,2,32,1024]{3,2,1,0:T(8,128)(2,1)} %constant_dynamic-update-slice_fusion.16), calls=%async_computation.2 | async-start | bytes 2097152 | tf_op jit(solution)/shard_map/all_to_all | solution.py:13
  77.1 2.3 %copy.43 = bf16[2,8,32,1024]{3,2,1,0:T(8,128)(2,1)} copy(bf16[2,8,32,1024]{3,2,0,1:T(8,128)(2,1)} %bitcast.94) | data formatting | bytes 2097152 | tf_op jit(solution)/shard_map/reshape | solution.py:14
  79.4 1.5 collective-permute-start.2
  80.9 2.3 %copy.44 = bf16[2,8,32,1024]{3,2,1,0:T(8,128)(2,1)} copy(bf16[2,8,32,1024]{3,2,0,1:T(8,128)(2,1)} %bitcast.28) | data formatting | bytes 2097152 | tf_op jit(solution)/shard_map/reshape | solution.py:14
  83.7 18.0 %all-to-all-done.2 = bf16[8,2,32,1024]{3,2,1,0:T(8,128)(2,1)} async-done(((bf16[8,2,32,1024]{3,2,1,0:T(8,128)(2,1)}), bf16[8,2,32,1024]{3,2,1,0:T(8,128)(2,1)}, u32[]{:S(2)}, u32[]{:S(2)}) %all-to-all-start.2) | async-done | bytes 1048608 | tf_op jit(solution)/shard_map/all_to_all | solution.py:13
  101.8 2.3 %copy.45 = bf16[8,2,32,1024]{3,2,0,1:T(8,128)(2,1)} copy(bf16[8,2,32,1024]{3,2,1,0:T(8,128)(2,1)} %all-to-all-done.2) | data formatting | bytes 2097152 | tf_op jit(solution)/shard_map/all_to_all | solution.py:13
  104.1 1.5 collective-permute-start.4
  105.6 4.3 %fusion.59 = f32[2,256,704]{1,2,0:T(8,128)} fusion(bf16[2,256,1024]{2,1,0:T(8,128)(2,1)} %bitcast.18, bf16[2,1024,704]{1,2,0:T(8,128)(2,1)} %param.23), kind=kOutput, calls=%fused_computation.99 | convolution fusion | flops 738197504 | bytes 5373952 | tf_op jit(solution)/shard_map/erd,edf->erf/dot_general | solution.py:49
  109.9 3.3 %fusion.60 = f32[2,256,704]{1,2,0:T(8,128)} fusion(bf16[2,256,1024]{2,1,0:T(8,128)(2,1)} %bitcast.29, bf16[2,1024,704]{1,2,0:T(8,128)(2,1)S(1)} %copy-done.1), kind=kOutput, calls=%fused_computation.100 | convolution fusion | flops 738197504 | bytes 5373952 | tf_op jit(solution)/shard_map/erd,edf->erf/dot_general | solution.py:50
  113.2 7.3 %fusion.6 = f32[2,256,1024]{2,1,0:T(8,128)} fusion(bf16[2,1024,704]{1,2,0:T(8,128)(2,1)} %param.23, bf16[2,256,1024]{2,1,0:T(8,128)(2,1)} %bitcast.40, bf16[2,1024,704]{1,2,0:T(8,128)(2,1)} %param.24, f32[2,256,704]{1,2,0:T(8,128)} %fusion.59, f32[2,256,704]{1,2,0:T(8,128)} %fusion.60), kind=kOutput, calls=%fused_computation.23 | convolution fusion | flops 1480720384 | bytes 11796480 | tf_op jit(solution)/shard_map/erf,edf->erd/dot_general | solution.py:55
  120.5 4.3 %fusion.61 = f32[2,256,704]{1,2,0:T(8,128)} fusion(bf16[2,256,1024]{2,1,0:T(8,128)(2,1)} %bitcast.18, bf16[2,1024,704]{1,2,0:T(8,128)(2,1)} %collective-permute-done), kind=kOutput, calls=%fused_computation.101 | convolution fusion | flops 738197504 | bytes 5373952 | tf_op jit(solution)/shard_map/erd,edf->erf/dot_general | solution.py:49
  124.8 3.3 %fusion.63 = f32[2,256,704]{1,2,0:T(8,128)} fusion(bf16[2,256,1024]{2,1,0:T(8,128)(2,1)} %collective-permute-done.2, bf16[2,1024,704]{1,2,0:T(8,128)(2,1)S(1)} %copy-done.2), kind=kOutput, calls=%fused_computation.103 | convolution fusion | flops 738197504 | bytes 5373952 | tf_op jit(solution)/shard_map/erd,edf->erf/dot_general | solution.py:49
  128.1 4.2 %fusion.65 = f32[2,256,704]{1,2,0:T(8,128)} fusion(bf16[2,256,1024]{2,1,0:T(8,128)(2,1)} %collective-permute-done.2, bf16[2,1024,704]{1,2,0:T(8,128)(2,1)} %collective-permute-done), kind=kOutput, calls=%fused_computation.105 | convolution fusion | flops 738197504 | bytes 5373952 | tf_op jit(solution)/shard_map/erd,edf->erf/dot_general | solution.py:49
  132.4 3.3 %fusion.64 = f32[2,256,704]{1,2,0:T(8,128)} fusion(bf16[2,256,1024]{2,1,0:T(8,128)(2,1)} %collective-permute-done.3, bf16[2,1024,704]{1,2,0:T(8,128)(2,1)S(1)} %copy-done.2), kind=kOutput, calls=%fused_computation.104 | convolution fusion | flops 738197504 | bytes 5373952 | tf_op jit(solution)/shard_map/erd,edf->erf/dot_general | solution.py:50
  135.6 4.2 %fusion.66 = f32[2,256,704]{1,2,0:T(8,128)} fusion(bf16[2,256,1024]{2,1,0:T(8,128)(2,1)} %collective-permute-done.3, bf16[2,1024,704]{1,2,0:T(8,128)(2,1)} %collective-permute-done), kind=kOutput, calls=%fused_computation.106 | convolution fusion | flops 738197504 | bytes 5373952 | tf_op jit(solution)/shard_map/erd,edf->erf/dot_general | solution.py:50
  139.8 10.0 %collective-permute-done.4 = bf16[2,256,1024]{2,1,0:T(8,128)(2,1)} collective-permute-done((bf16[2,256,1024]{2,1,0:T(8,128)(2,1)}, bf16[2,256,1024]{2,1,0:T(8,128)(2,1)}, u32[]{:S(2)}, u32[]{:S(2)}) %collective-permute-start.4) | collective-permute-done | bytes 1048608 | tf_op jit(solution)/shard_map/ppermute | solution.py:117
  149.8 7.4 %fusion.14 = f32[2,256,1024]{2,1,0:T(8,128)} fusion(bf16[2,1024,704]{1,2,0:T(8,128)(2,1)} %param.23, f32[2,256,704]{1,2,0:T(8,128)} %fusion.63, f32[2,256,704]{1,2,0:T(8,128)} %fusion.64, bf16[2,256,1024]{2,1,0:T(8,128)(2,1)} %collective-permute-done.4, bf16[2,1024,704]{1,2,0:T(8,128)(2,1)} %param.24), kind=kOutput, calls=%fused_computation.32 | convolution fusion | flops 1480720384 | bytes 11796480 | tf_op jit(solution)/shard_map/erf,edf->erd/dot_general | solution.py:55
  157.2 7.8 %add_convert_fusion.1 = bf16[2,256,1024]{2,1,0:T(8,128)(2,1)} fusion(f32[2,256,1024]{2,1,0:T(8,128)} %fusion.14, bf16[2,1024,704]{1,2,0:T(8,128)(2,1)} %collective-permute-done, f32[2,256,704]{1,2,0:T(8,128)} %fusion.65, f32[2,256,704]{1,2,0:T(8,128)} %fusion.66, bf16[2,256,1024]{2,1,0:T(8,128)(2,1)} %collective-permute-done.4, ...), kind=kOutput, calls=%fused_computation.2 | convolution fusion | flops 1481768960 | bytes 12845056 | tf_op jit(solution)/shard_map/erf,edf->erd/dot_general | solution.py:55
  165.0 1.5 collective-permute-start.5
  166.5 4.2 %fusion.62 = f32[2,256,704]{1,2,0:T(8,128)} fusion(bf16[2,256,1024]{2,1,0:T(8,128)(2,1)} %bitcast.29, bf16[2,1024,704]{1,2,0:T(8,128)(2,1)} %collective-permute-done), kind=kOutput, calls=%fused_computation.102 | convolution fusion | flops 738197504 | bytes 5373952 | tf_op jit(solution)/shard_map/erd,edf->erf/dot_general | solution.py:50
  170.7 7.4 %fusion.13 = f32[2,256,1024]{2,1,0:T(8,128)} fusion(bf16[2,1024,704]{1,2,0:T(8,128)(2,1)} %collective-permute-done, f32[2,256,704]{1,2,0:T(8,128)} %fusion.61, f32[2,256,704]{1,2,0:T(8,128)} %fusion.62, bf16[2,256,1024]{2,1,0:T(8,128)(2,1)} %bitcast.40, bf16[2,1024,704]{1,2,0:T(8,128)(2,1)} %collective-permute-done.1), kind=kOutput, calls=%fused_computation.31 | convolution fusion | flops 1480720384 | bytes 11796480 | tf_op jit(solution)/shard_map/erf,edf->erd/dot_general | solution.py:55
  178.1 11.5 %collective-permute-done.5 = bf16[2,256,1024]{2,1,0:T(8,128)(2,1)} collective-permute-done((bf16[2,256,1024]{2,1,0:T(8,128)(2,1)}, bf16[2,256,1024]{2,1,0:T(8,128)(2,1)}, u32[]{:S(2)}, u32[]{:S(2)}) %collective-permute-start.5) | collective-permute-done | bytes 1048608 | tf_op jit(solution)/shard_map/ppermute | solution.py:122
  189.6 3.1 %add_convert_fusion = bf16[2,256,1024]{2,1,0:T(8,128)(2,1)S(1)} fusion(bf16[2,256,1024]{2,1,0:T(8,128)(2,1)} %collective-permute-done.5, f32[2,256,1024]{2,1,0:T(8,128)} %fusion.6, f32[2,256,1024]{2,1,0:T(8,128)} %fusion.13), kind=kLoop, calls=%fused_computation.1 | loop fusion | flops 2097152 | bytes 6291456 | tf_op jit(solution)/shard_map/convert_element_type | solution.py:124
  192.7 1.1 copy.46
  193.8 29.5 %all_to_all.30 = bf16[2,256,1024]{2,0,1:T(2,128)(2,1)S(1)} all-to-all(bf16[2,256,1024]{2,0,1:T(2,128)(2,1)S(1)} %copy.46), channel_id=1, replica_groups=mesh['expert'=8,'dp'=4] {'expert'}, dimensions={1} | all-to-all | bytes 2097152 | tf_op jit(solution)/shard_map/all_to_all | solution.py:123
  223.7 1.3 fusion.5
  (31 shorter events, 2.3 us)
Async XLA Ops:
  0.0 48.7 %copy-start = (bf16[1024,1024]{1,0:T(8,128)(2,1)S(1)}, bf16[1024,1024]{1,0:T(8,128)(2,1)}, u32[]{:S(2)}) copy-start(bf16[1024,1024]{1,0:T(8,128)(2,1)} %param.25) | copy-start | bytes 6291460
  3.8 12.7 %copy-start.4 = (bf16[1,1,128,1024]{3,2,1,0:T(8,128)(2,1)S(1)}, bf16[1,1,128,1024]{3,2,1,0:T(8,128)(2,1)}, u32[]{:S(2)}) copy-start(bf16[1,1,128,1024]{3,2,1,0:T(8,128)(2,1)} %param.17) | copy-start | bytes 786436
  9.1 12.8 %copy-start.6 = (f32[1024]{0:T(1024)S(1)}, f32[1024]{0:T(1024)}, u32[]{:S(2)}) copy-start(f32[1024]{0:T(1024)} %param.22) | copy-start | bytes 12292
  9.1 33.2 %all-to-all-start = ((bf16[8,2,32,1024]{3,2,1,0:T(8,128)(2,1)}), bf16[8,2,32,1024]{3,2,1,0:T(8,128)(2,1)S(1)}, u32[]{:S(2)}, u32[]{:S(2)}) async-start(bf16[8,2,32,1024]{3,2,1,0:T(8,128)(2,1)} %constant_dynamic-update-slice_fusion), calls=%async_computation | async-start | bytes 2097152 | tf_op jit(solution)/shard_map/all_to_all | solution.py:13
  28.8 17.7 %copy-start.5 = (bf16[1,1,128,1024]{2,3,1,0:T(8,128)(2,1)S(1)}, bf16[1,1,128,1024]{2,3,1,0:T(8,128)(2,1)}, u32[]{:S(2)}) copy-start(bf16[1,1,128,1024]{2,3,1,0:T(8,128)(2,1)} %copy.42) | copy-start | bytes 786436
  42.3 6.4 %copy-start.3 = (bf16[8,2,32,1024]{3,2,1,0:T(8,128)(2,1)}, bf16[8,2,32,1024]{3,2,1,0:T(8,128)(2,1)S(1)}, u32[]{:S(2)}) copy-start(bf16[8,2,32,1024]{3,2,1,0:T(8,128)(2,1)S(1)} %all-to-all-done) | copy-start | bytes 3145732
  42.3 29.8 %all-to-all-start.1 = ((bf16[8,2,32,1024]{3,2,1,0:T(8,128)(2,1)}), bf16[8,2,32,1024]{3,2,1,0:T(8,128)(2,1)}, u32[]{:S(2)}, u32[]{:S(2)}) async-start(bf16[8,2,32,1024]{3,2,1,0:T(8,128)(2,1)} %constant_dynamic-update-slice_fusion.8), calls=%async_computation.1 | async-start | bytes 2097152 | tf_op jit(solution)/shard_map/all_to_all | solution.py:13
  48.7 0.8 copy-start.7
  72.1 29.7 %all-to-all-start.2 = ((bf16[8,2,32,1024]{3,2,1,0:T(8,128)(2,1)}), bf16[8,2,32,1024]{3,2,1,0:T(8,128)(2,1)}, u32[]{:S(2)}, u32[]{:S(2)}) async-start(bf16[8,2,32,1024]{3,2,1,0:T(8,128)(2,1)} %constant_dynamic-update-slice_fusion.16), calls=%async_computation.2 | async-start | bytes 2097152 | tf_op jit(solution)/shard_map/all_to_all | solution.py:13
  76.5 44.0 %collective-permute-start = (bf16[2,1024,704]{1,2,0:T(8,128)(2,1)}, bf16[2,1024,704]{1,2,0:T(8,128)(2,1)}, u32[]{:S(2)}, u32[]{:S(2)}) collective-permute-start(bf16[2,1024,704]{1,2,0:T(8,128)(2,1)} %param.23), channel_id=1, source_target_pairs={{0,1},{1,0},{2,3},{3,2},{4,5},{5,4},{6,7},{7,6},{8,9},{9,8},{10,11... | collective-permute-start | bytes 8650760 | tf_op jit(solution)/shard_map/ppermute | solution.py:83
  76.6 80.6 %collective-permute-start.1 = (bf16[2,1024,704]{1,2,0:T(8,128)(2,1)}, bf16[2,1024,704]{1,2,0:T(8,128)(2,1)}, u32[]{:S(2)}, u32[]{:S(2)}) collective-permute-start(bf16[2,1024,704]{1,2,0:T(8,128)(2,1)} %param.24), channel_id=1, source_target_pairs={{0,1},{1,0},{2,3},{3,2},{4,5},{5,4},{6,7},{7,6},{8,9},{9,8},{10,11... | collective-permute-start | bytes 8650760 | tf_op jit(solution)/shard_map/ppermute | solution.py:83
  79.4 45.4 %collective-permute-start.2 = (bf16[2,256,1024]{2,1,0:T(8,128)(2,1)}, bf16[2,256,1024]{2,1,0:T(8,128)(2,1)}, u32[]{:S(2)}, u32[]{:S(2)}) collective-permute-start(bf16[2,256,1024]{2,1,0:T(8,128)(2,1)} %bitcast.18), channel_id=1, source_target_pairs={{0,2},{1,3},{2,0},{3,1},{4,6},{5,7},{6,4},{7,5},{8,10},{9,11},{10,... | collective-permute-start | bytes 3145736 | tf_op jit(solution)/shard_map/ppermute | solution.py:117
  83.2 49.1 %collective-permute-start.3 = (bf16[2,256,1024]{2,1,0:T(8,128)(2,1)}, bf16[2,256,1024]{2,1,0:T(8,128)(2,1)}, u32[]{:S(2)}, u32[]{:S(2)}) collective-permute-start(bf16[2,256,1024]{2,1,0:T(8,128)(2,1)} %bitcast.29), channel_id=1, source_target_pairs={{0,2},{1,3},{2,0},{3,1},{4,6},{5,7},{6,4},{7,5},{8,10},{9,11},{10,... | collective-permute-start | bytes 3145736 | tf_op jit(solution)/shard_map/ppermute | solution.py:117
  104.1 5.8 %copy-start.1 = (bf16[2,1024,704]{1,2,0:T(8,128)(2,1)S(1)}, bf16[2,1024,704]{1,2,0:T(8,128)(2,1)}, u32[]{:S(2)}) copy-start(bf16[2,1024,704]{1,2,0:T(8,128)(2,1)} %param.23) | copy-start | bytes 8650756
  104.1 45.7 %collective-permute-start.4 = (bf16[2,256,1024]{2,1,0:T(8,128)(2,1)}, bf16[2,256,1024]{2,1,0:T(8,128)(2,1)}, u32[]{:S(2)}, u32[]{:S(2)}) collective-permute-start(bf16[2,256,1024]{2,1,0:T(8,128)(2,1)} %bitcast.40), channel_id=1, source_target_pairs={{0,2},{1,3},{2,0},{3,1},{4,6},{5,7},{6,4},{7,5},{8,10},{9,11},{10,... | collective-permute-start | bytes 3145736 | tf_op jit(solution)/shard_map/ppermute | solution.py:117
  120.5 4.3 %copy-start.2 = (bf16[2,1024,704]{1,2,0:T(8,128)(2,1)S(1)}, bf16[2,1024,704]{1,2,0:T(8,128)(2,1)}, u32[]{:S(2)}) copy-start(bf16[2,1024,704]{1,2,0:T(8,128)(2,1)} %param.23) | copy-start | bytes 8650756
  165.0 24.6 %collective-permute-start.5 = (bf16[2,256,1024]{2,1,0:T(8,128)(2,1)}, bf16[2,256,1024]{2,1,0:T(8,128)(2,1)}, u32[]{:S(2)}, u32[]{:S(2)}) collective-permute-start(bf16[2,256,1024]{2,1,0:T(8,128)(2,1)} %add_convert_fusion.1), channel_id=1, source_target_pairs={{2,0},{3,1},{0,2},{1,3},{6,4},{7,5},{4,6},{5,7},{10,8},{11,9},{8,1... | collective-permute-start | bytes 3145736 | tf_op jit(solution)/shard_map/ppermute | solution.py:122
